TPU v7x, 32 devices: a whole 2x2x4 slice. The times are simulated.
32 devices in a mesh: query: 8 (over z, y), tensor: 2 (over x), dp: 2 (over core).
Axes of the slice: x: 2, y: 2, z: 4, core: 2. Of those that a mesh axis runs over, the one named last changes fastest.
Arguments:
- hidden: bfloat16 [16, 1024, 14336], P(('query', 'dp'), None, 'tensor'), may hold values from -6 to 6
- out_grad: bfloat16 [16, 1024, 4096], P(('query', 'dp'), None, 'tensor'), may hold values from -6 to 6
- proj_in: bfloat16 [14336, 64], P('tensor'), may hold values from -0.046875 to 0.046875
- proj_out: bfloat16 [4096, 64], P('tensor'), may hold values from -0.09375 to 0.09375
- seg_ids: int32 [16, 1024], P(('query', 'dp')), may hold values from 0 to 31, never falling along the last dimension, each value on 1 to 288 neighbouring positions
- queries: bfloat16 [1024, 4096], P(('query', 'dp'), 'tensor'), may hold values from -0.01171875 to 0.01171875
Outputs:
- scores: float32 [512, 1024], P('tensor', ('query', 'dp'))
All inputs are finite; a program needn't handle non-finite values.
Results may differ from a plain program's by a relative error of at most 0.004.
Values may be sent and summed in bfloat16 or wider, within the bound.
No kernel may reach another device: no remote copies, remote signals or barrier semaphores. Data moves between devices by JAX's collectives and lax.ppermute only.
A program may use at most 64 MiB of HBM per device.

v0:
```python
import jax
import jax.numpy as jnp
from jax import lax
from jax.sharding import PartitionSpec as P

SEGS = 32


def local(hidden, out_grad, proj_in, proj_out, seg_ids, queries):
    tokens = hidden[0]
    grads = out_grad[0]
    segment = seg_ids[0]
    part_in = jnp.dot(tokens, proj_in, preferred_element_type=jnp.float32)
    part_out = jnp.dot(grads, proj_out, preferred_element_type=jnp.float32)
    act_proj = lax.psum(part_in, "tensor")
    grad_share = lax.psum_scatter(part_out, "tensor", scatter_dimension=1, tiled=True)
    outer = (
        (grad_share[:, :, None] * act_proj[:, None, :])
        .reshape(tokens.shape[0], -1)
        .astype(jnp.bfloat16)
    )
    member = (segment[None, :] == jnp.arange(SEGS, dtype=jnp.int32)[:, None]).astype(jnp.bfloat16)
    doc_feats = jnp.dot(member, outer, preferred_element_type=jnp.float32).astype(jnp.bfloat16)
    table = lax.dot_general(
        lax.all_gather(doc_feats, ("query", "dp"), axis=0, tiled=True),
        queries,
        (((1,), (1,)), ((), ())),
        preferred_element_type=jnp.float32,
    )
    return lax.psum_scatter(table, "tensor", scatter_dimension=0, tiled=True)


def solution(mesh):
    in_specs = (
        P(("query", "dp"), None, "tensor"),
        P(("query", "dp"), None, "tensor"),
        P("tensor", None),
        P("tensor", None),
        P(("query", "dp"), None),
        P(("query", "dp"), "tensor"),
    )
    out_specs = P("tensor", ("query", "dp"))
    return jax.shard_map(local, mesh=mesh, in_specs=in_specs, out_specs=out_specs, check_vma=False)
```

profile of v0, /device:TPU:0, one launch (start us, length us, event | category | flops | bytes accessed | tf_op | source)
XLA Modules:
  0.0 123.0 jit_solution(5992180469758918118)
XLA Ops:
  6.5 0.0 copy-start
  6.5 0.0 copy-start.1
  6.5 0.0 all-reduce.2.cloned.1.call-start
  6.5 1.2 copy-done
  7.7 10.4 %fusion = f32[1024,64]{0,1:T(8,128)} fusion(bf16[7168,64]{0,1:T(8,128)(2,1)S(1)} %copy-done, bf16[1,1024,7168]{2,1,0:T(8,128)(2,1)} %param.6), kind=kOutput, calls=%fused_computation | convolution fusion | flops 939524096 | bytes 15859712 | tf_op jit(solution)/shard_map/dot_general | solution.py:13
  18.1 0.0 all-reduce.2.cloned.1.call-update
  18.2 0.0 copy-start.3
  18.2 0.0 reduce-scatter.3.cloned.1.call-start
  18.2 0.0 copy-done.1
  18.2 4.3 %fusion.2 = f32[1024,64]{0,1:T(8,128)} fusion(bf16[2048,64]{0,1:T(8,128)(2,1)S(1)} %copy-done.1, bf16[1,1024,2048]{2,1,0:T(8,128)(2,1)} %param.7), kind=kOutput, calls=%fused_computation.3 | convolution fusion | flops 268435456 | bytes 4718592 | tf_op jit(solution)/shard_map/dot_general | solution.py:14
  22.5 0.0 reduce-scatter.3.cloned.1.call-update
  22.5 0.0 copy-start.2
  22.6 0.0 all-gather.2.cloned.1.call-start
  22.6 21.7 %all-reduce.2.cloned.1.call-done = f32[1024,64]{0,1:T(8,128)} async-done(((f32[1024,64]{0,1:T(8,128)}), f32[1024,64]{0,1:T(8,128)}) %all-reduce.2.cloned.1.call-update) | async-done | bytes 262160 | tf_op jit(solution)/shard_map/psum | solution.py:15
  44.3 14.0 %reduce-scatter.3.cloned.1.call-done = f32[1024,32]{0,1:T(8,128)} async-done(((f32[1024,64]{0,1:T(8,128)}), f32[1024,32]{0,1:T(8,128)}) %reduce-scatter.3.cloned.1.call-update) | async-done | bytes 131088 | tf_op jit(solution)/shard_map/reduce_scatter | solution.py:16
  58.4 2.2 %multiply_convert_fusion = bf16[1024,32,64]{0,2,1:T(8,128)(2,1)S(1)} fusion(f32[1024,64]{0,1:T(8,128)} %all-reduce.2.cloned.1.call-done, f32[1024,32]{0,1:T(8,128)} %reduce-scatter.3.cloned.1.call-done), kind=kLoop, calls=%fused_computation.2 | loop fusion | flops 4194304 | bytes 4587520 | tf_op jit(solution)/shard_map/convert_element_type | solution.py:20
  60.6 0.0 copy-done.3
  60.6 2.0 %convolution_convert_fusion = bf16[32,2048]{1,0:T(8,128)(2,1)} fusion(bf16[1024,2048]{0,1:T(8,128)(2,1)S(1)} %bitcast.13, s32[1024]{0:T(1024)S(1)} %bitcast.14), kind=kOutput, calls=%fused_computation.5 | convolution fusion | flops 134316032 | bytes 4329472 | tf_op jit(solution)/shard_map/dot_general | solution.py:23
  62.6 0.0 all-gather.2.cloned.1.call-update
  62.6 0.0 reduce-scatter.5.cloned.1.call-start
  62.7 41.6 %all-gather.2.cloned.1.call-done = bf16[512,2048]{1,0:T(8,128)(2,1)} async-done(((bf16[32,2048]{1,0:T(8,128)(2,1)}), bf16[512,2048]{1,0:T(8,128)(2,1)}) %all-gather.2.cloned.1.call-update) | async-done | bytes 2097168 | tf_op jit(solution)/shard_map/all_gather | solution.py:25
  104.2 0.0 copy-done.2
  104.2 3.0 %fusion.5 = f32[512,64]{0,1:T(8,128)} fusion(bf16[512,2048]{1,0:T(8,128)(2,1)} %all-gather.2.cloned.1.call-done, bf16[64,2048]{1,0:T(8,128)(2,1)S(1)} %copy-done.2), kind=kOutput, calls=%fused_computation.8 | convolution fusion | flops 134217728 | bytes 2490368 | tf_op jit(solution)/shard_map/dot_general | solution.py:24
  107.2 0.0 reduce-scatter.5.cloned.1.call-update
  107.3 9.2 %reduce-scatter.5.cloned.1.call-done = f32[256,64]{0,1:T(8,128)} async-done(((f32[512,64]{0,1:T(8,128)}), f32[256,64]{0,1:T(8,128)}) %reduce-scatter.5.cloned.1.call-update) | async-done | bytes 65552 | tf_op jit(solution)/shard_map/reduce_scatter | solution.py:30
Async XLA Ops:
  6.5 1.2 copy-start
  6.5 11.7 %copy-start.1 = (bf16[2048,64]{0,1:T(8,128)(2,1)S(1)}, bf16[2048,64]{0,1:T(8,128)(2,1)}, u32[]{:S(2)}) copy-start(bf16[2048,64]{0,1:T(8,128)(2,1)} %param.9) | copy-start | bytes 786436
  6.5 37.8 %all-reduce.2.cloned.1.call-start = ((), (), s32[]{:S(2)}) async-start(), calls=%async_computation.3 | async-start | bytes 524288 | tf_op jit(solution)/shard_map/psum | solution.py:15
  18.2 42.5 %copy-start.3 = (s32[1,1024]{1,0:T(1,128)S(1)}, s32[1,1024]{1,0:T(1,128)}, u32[]{:S(2)}) copy-start(s32[1,1024]{1,0:T(1,128)} %param.10) | copy-start | bytes 12292
  18.2 40.2 %reduce-scatter.3.cloned.1.call-start = ((), (), s32[]{:S(2)}) async-start(), calls=%async_computation.2 | async-start | bytes 393216 | tf_op jit(solution)/shard_map/reduce_scatter | solution.py:16
  22.5 81.7 %copy-start.2 = (bf16[64,2048]{1,0:T(8,128)(2,1)S(1)}, bf16[64,2048]{1,0:T(8,128)(2,1)}, u32[]{:S(2)}) copy-start(bf16[64,2048]{1,0:T(8,128)(2,1)} %param.11) | copy-start | bytes 786436
  22.6 81.7 %all-gather.2.cloned.1.call-start = ((), (), s32[]{:S(2)}) async-start(), calls=%async_computation.4 | async-start | bytes 2228224 | tf_op jit(solution)/shard_map/all_gather | solution.py:25
  62.6 53.9 %reduce-scatter.5.cloned.1.call-start = ((), (), s32[]{:S(2)}) async-start(), calls=%async_computation.5 | async-start | bytes 196608 | tf_op jit(solution)/shard_map/reduce_scatter | solution.py:30
Sparse Core Ops, SparseCore 0:
  18.3 26.0 all-reduce.1
  46.6 11.7 reduce-scatter.2
  62.7 41.4 all-gather.1
  107.4 9.0 reduce-scatter.4
where the time goes:
time: 123 us
  waiting for transfers between devices  86.6 us (70%)
  matrix products  19.7 us (16%)
  between operations  13.2 us (11%)
  other arithmetic  2.24 us (2%)
    all_gather x1, waiting for transfers between devices, local(): lax.all_gather(doc_feats, ('query', 'dp'), axis=0, tiled=True)  41.6 us
    psum x1, waiting for transfers between devices, local(): act_proj = lax.psum(part_in, 'tensor')  21.7 us
    reduce_scatter x1, waiting for transfers between devices, local(): lax.psum_scatter(part_out, 'tensor', scatter_dimension=1, tiled=True)  14 us
    dot_general x1, matrix products, local(): part_in = jnp.dot(tokens, proj_in, preferred_element_type=jnp.float32)  10.4 us
    reduce_scatter x1, waiting for transfers between devices, local(): return lax.psum_scatter(table, 'tensor', scatter_dimension=0, tiled=True)  9.23 us
    dot_general x1, matrix products, local(): part_out = jnp.dot(grads, proj_out, preferred_element_type=jnp.float32)  4.28 us
    dot_general x1, matrix products, local(): lax.dot_general(lax.all_gather(doc_feats, ('query', 'dp'), axis=0, tiled=...  3 us
  transfers between devices with their start and end apart: 4, of which 4 were waited for; matrix products, arithmetic and copies ran while one was open for 3% of the time, Pallas kernels for 0%

commit v1 on v0

v1 whole, which is shorter than its diff:
```python
import functools
import math

import jax
import jax.numpy as jnp
from jax import lax
from jax.experimental import pallas as pl
from jax.experimental.pallas import tpu as pltpu
from jax.sharding import PartitionSpec as P

SEGS = 32
MIB = 2**20
NT = (((1,), (1,)), ((), ()))
VMEM = pl.BlockSpec(memory_space=pltpu.VMEM)
SMEM = pl.BlockSpec(memory_space=pltpu.SMEM)
ANY = pl.BlockSpec(memory_space=pl.ANY)


def tiles(length, tile):
    return [(start, min(tile, length - start)) for start in range(0, length, tile)]


def project_kernel(parts, place, hidden, grads, w_in, w_out, keep, send, h_buf, g_buf, wi_buf, wo_buf, out_side, h_sem, g_sem, w_sem):
    length, width = h_buf.shape[0], w_in.shape[0]
    block = width // parts
    weights = [pltpu.make_async_copy(w_out, wo_buf, w_sem.at[0]), pltpu.make_async_copy(w_in, wi_buf, w_sem.at[1])]
    spans = tiles(length, 256)
    weights[0].start()
    copies = []
    for n, (start, size) in enumerate(spans):
        rows = pl.ds(start, size)
        copies.append(
            (
                pltpu.make_async_copy(grads.at[rows], g_buf.at[rows], g_sem.at[n]),
                pltpu.make_async_copy(hidden.at[rows], h_buf.at[rows], h_sem.at[n]),
            )
        )
    copies[0][0].start()
    weights[1].start()
    copies[0][1].start()
    for first, second in copies[1:]:
        first.start()
        second.start()
    for n, (start, size) in enumerate(spans):
        rows = slice(start, start + size)
        if n == 0:
            weights[0].wait()
        copies[n][0].wait()
        out_side[:, rows] = lax.dot_general(wo_buf[...], g_buf[rows], NT, preferred_element_type=jnp.float32)
        if n == 0:
            weights[1].wait()
        copies[n][1].wait()
        act = lax.dot_general(wi_buf[...], h_buf[rows], NT, preferred_element_type=jnp.float32)
        keep[:width, rows] = act
        for d in range(1, parts):
            send[d - 1, :width, rows] = act.astype(jnp.bfloat16)
    keep[width:] = out_side[pl.ds(pl.multiple_of(place[0] * block, block), block)]
    for d in range(1, parts):
        there = lax.rem(place[0] + d, parts)
        send[d - 1, width:] = out_side[pl.ds(pl.multiple_of(there * block, block), block)].astype(jnp.bfloat16)


def project(parts, place, hidden, grads, w_in, w_out):
    (length, units), features, width = hidden.shape, grads.shape[1], w_in.shape[0]
    rows, steps = width + width // parts, len(tiles(length, 256))
    return pl.pallas_call(
        functools.partial(project_kernel, parts),
        out_shape=(
            jax.ShapeDtypeStruct((rows, length), jnp.float32),
            jax.ShapeDtypeStruct((max(parts - 1, 1), rows, length), jnp.bfloat16),
        ),
        in_specs=[SMEM, ANY, ANY, ANY, ANY],
        out_specs=(VMEM, VMEM),
        scratch_shapes=[
            pltpu.VMEM((length, units), jnp.bfloat16),
            pltpu.VMEM((length, features), jnp.bfloat16),
            pltpu.VMEM((width, units), jnp.bfloat16),
            pltpu.VMEM((width, features), jnp.bfloat16),
            pltpu.VMEM((width, length), jnp.float32),
            pltpu.SemaphoreType.DMA((steps,)),
            pltpu.SemaphoreType.DMA((steps,)),
            pltpu.SemaphoreType.DMA((2,)),
        ],
        compiler_params=pltpu.CompilerParams(vmem_limit_bytes=40 * MIB),
        name="project",
    )(place, hidden, grads, w_in, w_out)


def features_kernel(width, segment, keep, *rest):
    received, out = rest[:-1], rest[-1]
    total = keep[...]
    for other in received:
        total = total + other[...].astype(jnp.float32)
    act, side = total[:width], total[width:]
    block, length = side.shape
    docs = lax.broadcasted_iota(jnp.int32, (SEGS, length), 0)
    member = (docs == segment[...]).astype(jnp.bfloat16)
    group = math.gcd(4, block)
    for start in range(0, block, group):
        outer = jnp.concatenate([(side[i : i + 1] * act).astype(jnp.bfloat16) for i in range(start, start + group)], axis=0)
        sums = lax.dot_general(member, outer, NT, preferred_element_type=jnp.float32)
        out[:, start * width : (start + group) * width] = sums.astype(jnp.bfloat16)


def features(width, segment, keep, received):
    block = keep.shape[0] - width
    return pl.pallas_call(
        functools.partial(features_kernel, width),
        out_shape=jax.ShapeDtypeStruct((SEGS, block * width), jnp.bfloat16),
        in_specs=[VMEM] * (2 + len(received)),
        out_specs=VMEM,
        compiler_params=pltpu.CompilerParams(vmem_limit_bytes=40 * MIB),
        name="features",
    )(segment, keep, *received)


def scores_kernel(parts, members, cores, place, *rest):
    count = members * cores
    blocks, queries = rest[:count], rest[count : count + parts]
    outs, table = rest[count + parts : count + 2 * parts], rest[-1]
    x, h, g, core = place[0], place[1], place[2], place[3]
    for d in range(members):
        for e in range(cores):
            at = holds(g, d, members) * cores + holds(core, e, cores)
            table[pl.ds(pl.multiple_of(at * SEGS, SEGS), SEGS)] = blocks[d * cores + e][...]
    for k in range(parts):
        which = lax.rem(h - x - k + 2 * parts, parts)
        chosen = queries[0][...]
        for d in range(1, parts):
            chosen = jnp.where(which == d, queries[d][...], chosen)
        outs[k][...] = lax.dot_general(chosen, table[...], NT, preferred_element_type=jnp.float32)


def scores(parts, members, cores, place, blocks, queries):
    docs, width = SEGS * len(blocks), blocks[0].shape[1]
    own = queries[0].shape[0]
    return pl.pallas_call(
        functools.partial(scores_kernel, parts, members, cores),
        out_shape=(jax.ShapeDtypeStruct((own, docs), jnp.float32),) * parts,
        in_specs=[SMEM] + [VMEM] * (len(blocks) + parts),
        out_specs=(VMEM,) * parts,
        scratch_shapes=[pltpu.VMEM((docs, width), jnp.bfloat16)],
        compiler_params=pltpu.CompilerParams(vmem_limit_bytes=40 * MIB),
        name="scores",
    )(place, *blocks, *queries)


def sends_to(i, d, size):
    return i ^ d if size & (size - 1) == 0 else (i + d) % size


def holds(i, d, size):
    return i ^ d if size & (size - 1) == 0 else lax.rem(i - d + size, size)


def local(rows_axis, parts, cores, hidden, out_grad, proj_in, proj_out, seg_ids, queries):
    members = rows_axis // parts
    x, q, core = lax.axis_index("tensor"), lax.axis_index("query"), lax.axis_index("dp")
    h, g = q // members, lax.rem(q, members)
    place = jnp.stack([x, h, g, core]).astype(jnp.int32)
    width = proj_in.shape[1]
    around = range(parts)
    asked = [queries]
    for d in range(1, parts):
        pairs = [(a * members + m, (a + d) % parts * members + m) for a in around for m in range(members)]
        asked.append(lax.ppermute(queries, "query", pairs))
    keep, send = project(parts, place, hidden[0], out_grad[0], proj_in.T, proj_out.T)
    received = []
    for d in range(1, parts):
        received.append(lax.ppermute(send[d - 1], "tensor", [(a, (a + d) % parts) for a in around]))
    own = features(width, seg_ids, keep, received)
    blocks = []
    for d in range(members):
        pairs = [(a * members + m, a * members + sends_to(m, d, members)) for a in around for m in range(members)]
        block = lax.ppermute(own, "query", pairs) if d else own
        for e in range(cores):
            pairs = [(c, sends_to(c, e, cores)) for c in range(cores)]
            blocks.append(lax.ppermute(block, "dp", pairs) if e else block)
    partial = scores(parts, members, cores, place, blocks, asked)
    total = None
    for k in range(parts):
        routes = [(a * members + m, b, (b + k) % parts * members + m, a) for a in around for m in range(members) for b in around]
        pairs = [(s * parts + b, t * parts + a) for s, b, t, a in routes if (s, b) != (t, a)]
        arrived = lax.ppermute(partial[k], ("query", "tensor"), pairs)
        at_home = (x == h) & (lax.rem(x + k, parts) == h)
        arrived = jnp.where(at_home, partial[k], arrived) if len(pairs) < len(routes) else arrived
        total = arrived if total is None else total + arrived
    return total.T


def solution(mesh):
    in_specs = (
        P(("query", "dp"), None, "tensor"),
        P(("query", "dp"), None, "tensor"),
        P("tensor", None),
        P("tensor", None),
        P(("query", "dp"), None),
        P(("query", "dp"), "tensor"),
    )
    out_specs = P("tensor", ("query", "dp"))
    step = functools.partial(local, mesh.shape["query"], mesh.shape["tensor"], mesh.shape["dp"])
    return jax.shard_map(step, mesh=mesh, in_specs=in_specs, out_specs=out_specs, check_vma=False)
```

time: 123 us -> 53.8 us (0.44)
  the two profiles are of different devices: /device:TPU:0 before, /device:TPU:2 now
where the time goes in v1:
time: 53.8 us; the launch traced here: 53.5 us
  waiting for transfers between devices  20.7 us (38%)
  Pallas kernels  15.8 us (29%)
  starting transfers between devices  12 us (22%)
  local copies, waits for them, and re-layouts  4.32 us (8%)
  other arithmetic  0.72 us (1%)
    pallas_call x1, Pallas kernels, project(): pl.pallas_call(functools.partial(project_kernel, parts), out_shape=(jax.S...  13.1 us
    ppermute x3, waiting for transfers between devices, local(): block = lax.ppermute(own, 'query', pairs) if d else own  7.4 us
    ppermute x1, waiting for transfers between devices, local(): lax.ppermute(send[d - 1], 'tensor', [(a, (a + d) % parts) for a in around])  6.63 us
    ppermute x2, starting transfers between devices, local(): arrived = lax.ppermute(partial[k], ('query', 'tensor'), pairs)  5.27 us
    ppermute x2, waiting for transfers between devices, local(): arrived = lax.ppermute(partial[k], ('query', 'tensor'), pairs)  4.64 us
    unnamed x10, local copies, waits for them, and re-layouts  4.32 us
    ppermute x3, starting transfers between devices, local(): block = lax.ppermute(own, 'query', pairs) if d else own  3.52 us
    ppermute x1, starting transfers between devices, local(): asked.append(lax.ppermute(queries, 'query', pairs))  2.59 us
  transfers between devices with their start and end apart: 11, of which 6 were waited for; matrix products, arithmetic and copies ran while one was open for 0% of the time, Pallas kernels for 0%

profile of v1, /device:TPU:2, one launch (start us, length us, event | category | flops | bytes accessed | tf_op | source)
XLA Modules:
  0.0 53.5 jit_solution(12292369331288415644)
XLA Ops:
  0.0 0.0 copy-start.4
  0.0 0.1 pad_add_fusion.place
  0.1 0.0 copy-start
  0.1 2.2 %copy-done = bf16[1,1024,2048]{2,1,0:T(8,128)(2,1)S(1)} copy-done((bf16[1,1024,2048]{2,1,0:T(8,128)(2,1)S(1)}, bf16[1,1024,2048]{2,1,0:T(8,128)(2,1)}, u32[]{:S(2)}) %copy-start) | copy-done | bytes 4194328
  2.3 0.0 copy-start.1
  2.3 1.2 %copy-done.1 = bf16[7168,64]{0,1:T(8,128)(2,1)S(1)} copy-done((bf16[7168,64]{0,1:T(8,128)(2,1)S(1)}, bf16[7168,64]{0,1:T(8,128)(2,1)}, u32[]{:S(2)}) %copy-start.1) | copy-done | bytes 917528
  3.4 0.0 copy-start.2
  3.5 0.9 %copy-done.2 = bf16[2048,64]{0,1:T(8,128)(2,1)S(1)} copy-done((bf16[2048,64]{0,1:T(8,128)(2,1)S(1)}, bf16[2048,64]{0,1:T(8,128)(2,1)}, u32[]{:S(2)}) %copy-start.2) | copy-done | bytes 262168
  4.4 0.0 copy-start.3
  4.4 13.1 %project.1 = (f32[96,1024]{1,0:T(8,128)S(1)}, bf16[1,96,1024]{2,1,0:T(8,128)(2,1)S(1)}) custom-call(s32[4]{0:T(128)S(1)} %pad_add_fusion.place, bf16[1024,7168]{1,0:T(8,128)(2,1)} %bitcast.15, bf16[1024,2048]{1,0:T(8,128)(2,1)S(1)} %bitcast.11, bf16[64,7168]{1,0:T(8,128)(2,1)S(1)} %bitcast.12, bf16[64,2048]{1,0:T(8,128)(2,1)S(1)} %bitcast.13), custom_call_target="tpu_custom_call" | custom-call | tf_op jit(solution)/shard_map/project/pallas_call | solution.py:66
  17.5 0.1 collective-permute-start
  17.6 6.6 %collective-permute-done.rest_0_ = bf16[96,1024]{1,0:T(8,128)(2,1)S(1)} collective-permute-done((bf16[96,1024]{1,0:T(8,128)(2,1)S(1)}, bf16[96,1024]{1,0:T(8,128)(2,1)S(1)}, u32[]{:S(2)}, u32[]{:S(2)}) %collective-permute-start) | collective-permute-done | bytes 196640 | tf_op jit(solution)/shard_map/ppermute | solution.py:170
  24.2 0.0 copy-done.4
  24.2 1.3 %features.1.rest_0_ = bf16[32,2048]{1,0:T(8,128)(2,1)S(1)} custom-call(s32[1,1024]{1,0:T(1,128)S(1)} %copy-done.4, f32[96,1024]{1,0:T(8,128)S(1)} %get-tuple-element.9.keep, bf16[96,1024]{1,0:T(8,128)(2,1)S(1)} %collective-permute-done.rest_0_), custom_call_target="tpu_custom_call" | custom-call | tf_op jit(solution)/shard_map/features/pallas_call | solution.py:107
  25.5 2.6 %collective-permute-start.6 = (bf16[32,2048]{1,0:T(8,128)(2,1)S(1)}, bf16[32,2048]{1,0:T(8,128)(2,1)S(1)}, u32[]{:S(2)}, u32[]{:S(2)}) collective-permute-start(bf16[32,2048]{1,0:T(8,128)(2,1)S(1)} %features.1.rest_0_), channel_id=1, source_target_pairs={{0,12},{4,8},{8,4},{12,0},{16,28},{20,24},{24,20},{28,16},{1,13},{... | collective-permute-start | bytes 393224 | tf_op jit(solution)/shard_map/ppermute | solution.py:175
  28.1 0.0 copy-done.3
  28.1 2.6 %collective-permute-start.8 = (bf16[64,2048]{1,0:T(8,128)(2,1)S(1)}, bf16[64,2048]{1,0:T(8,128)(2,1)S(1)}, u32[]{:S(2)}, u32[]{:S(2)}) collective-permute-start(bf16[64,2048]{1,0:T(8,128)(2,1)S(1)} %copy-done.3), channel_id=1, source_target_pairs={{0,16},{4,20},{8,24},{12,28},{16,0},{20,4},{24,8},{28,12},{1,17},{... | collective-permute-start | bytes 786440 | tf_op jit(solution)/shard_map/ppermute | solution.py:166
  30.7 0.4 collective-permute-start.4
  31.1 0.5 collective-permute-start.2
  31.7 0.0 collective-permute-start.1
  31.7 3.4 %collective-permute-done.6.rest_6_ = bf16[32,2048]{1,0:T(8,128)(2,1)S(1)} collective-permute-done((bf16[32,2048]{1,0:T(8,128)(2,1)S(1)}, bf16[32,2048]{1,0:T(8,128)(2,1)S(1)}, u32[]{:S(2)}, u32[]{:S(2)}) %collective-permute-start.6) | collective-permute-done | bytes 131104 | tf_op jit(solution)/shard_map/ppermute | solution.py:175
  35.1 0.0 collective-permute-start.7
  35.1 4.0 %collective-permute-done.4.rest_4_ = bf16[32,2048]{1,0:T(8,128)(2,1)S(1)} collective-permute-done((bf16[32,2048]{1,0:T(8,128)(2,1)S(1)}, bf16[32,2048]{1,0:T(8,128)(2,1)S(1)}, u32[]{:S(2)}, u32[]{:S(2)}) %collective-permute-start.4) | collective-permute-done | bytes 131104 | tf_op jit(solution)/shard_map/ppermute | solution.py:175
  39.1 0.0 collective-permute-start.5
  39.1 0.0 collective-permute-done.2.rest_2_
  39.1 0.5 collective-permute-start.3
  39.6 2.0 %collective-permute-done.8.rest_9_ = bf16[64,2048]{1,0:T(8,128)(2,1)S(1)} collective-permute-done((bf16[64,2048]{1,0:T(8,128)(2,1)S(1)}, bf16[64,2048]{1,0:T(8,128)(2,1)S(1)}, u32[]{:S(2)}, u32[]{:S(2)}) %collective-permute-start.8) | collective-permute-done | bytes 262176 | tf_op jit(solution)/shard_map/ppermute | solution.py:166
  41.6 0.0 collective-permute-done.1.rest_1_
  41.6 0.0 collective-permute-done.7.rest_7_
  41.6 0.0 collective-permute-done.5.rest_5_
  41.6 0.0 collective-permute-done.3.rest_3_
  41.6 1.4 %scores.1 = (f32[64,256]{1,0:T(8,128)S(1)}, f32[64,256]{1,0:T(8,128)S(1)}) custom-call(s32[4]{0:T(128)S(1)} %pad_add_fusion.place, bf16[32,2048]{1,0:T(8,128)(2,1)S(1)} %features.1.rest_0_, bf16[32,2048]{1,0:T(8,128)(2,1)S(1)} %collective-permute-done.1.rest_1_, bf16[32,2048]{1,0:T(8,128)(2,1)S(1)} %collective-permute-done.2.rest_2_, ...), custom_call_target="tpu_custom_call" | custom-call | tf_op jit(solution)/shard_map/scores/pallas_call | solution.py:137
  43.0 0.6 %collective-permute-start.10 = (f32[64,256]{1,0:T(8,128)S(1)}, f32[64,256]{1,0:T(8,128)S(1)}, u32[]{:S(2)}, u32[]{:S(2)}) collective-permute-start(f32[64,256]{1,0:T(8,128)S(1)} %get-tuple-element.12), channel_id=1, source_target_pairs={{0,16},{2,0},{4,20},{6,4},{8,24},{10,8},{12,28},{14,12},{16,18},{1... | collective-permute-start | bytes 196616 | tf_op jit(solution)/shard_map/ppermute | solution.py:184
  43.6 4.7 %collective-permute-start.9 = (f32[64,256]{1,0:T(8,128)S(1)}, f32[64,256]{1,0:T(8,128)S(1)}, u32[]{:S(2)}, u32[]{:S(2)}) collective-permute-start(f32[64,256]{1,0:T(8,128)S(1)} %get-tuple-element.11), channel_id=1, source_target_pairs={{2,16},{6,20},{10,24},{14,28},{16,2},{20,6},{24,10},{28,14},{3,17}... | collective-permute-start | bytes 196616 | tf_op jit(solution)/shard_map/ppermute | solution.py:184
  48.3 1.3 %collective-permute-done.10 = f32[64,256]{1,0:T(8,128)S(1)} collective-permute-done((f32[64,256]{1,0:T(8,128)S(1)}, f32[64,256]{1,0:T(8,128)S(1)}, u32[]{:S(2)}, u32[]{:S(2)}) %collective-permute-start.10) | collective-permute-done | bytes 65568 | tf_op jit(solution)/shard_map/ppermute | solution.py:184
  49.6 3.3 %collective-permute-done.9 = f32[64,256]{1,0:T(8,128)S(1)} collective-permute-done((f32[64,256]{1,0:T(8,128)S(1)}, f32[64,256]{1,0:T(8,128)S(1)}, u32[]{:S(2)}, u32[]{:S(2)}) %collective-permute-start.9) | collective-permute-done | bytes 65568 | tf_op jit(solution)/shard_map/ppermute | solution.py:184
  52.9 0.6 %add_bitcast_fusion = f32[256,64]{0,1:T(8,128)} fusion(f32[64,256]{1,0:T(8,128)S(1)} %collective-permute-done.10, f32[64,256]{1,0:T(8,128)S(1)} %get-tuple-element.11, f32[64,256]{1,0:T(8,128)S(1)} %collective-permute-done.9, pred[]{:T(512)S(6)} %and.13), kind=kLoop, calls=%fused_computation | loop fusion | flops 32768 | bytes 262145 | tf_op jit(solution)/shard_map/transpose | solution.py:188
Async XLA Ops:
  0.0 24.2 %copy-start.4 = (s32[1,1024]{1,0:T(1,128)S(1)}, s32[1,1024]{1,0:T(1,128)}, u32[]{:S(2)}) copy-start(s32[1,1024]{1,0:T(1,128)} %segment.1) | copy-start | bytes 12292
  0.1 2.2 %copy-start = (bf16[1,1024,2048]{2,1,0:T(8,128)(2,1)S(1)}, bf16[1,1024,2048]{2,1,0:T(8,128)(2,1)}, u32[]{:S(2)}) copy-start(bf16[1,1024,2048]{2,1,0:T(8,128)(2,1)} %param.7) | copy-start | bytes 12582916
  2.3 1.2 %copy-start.1 = (bf16[7168,64]{0,1:T(8,128)(2,1)S(1)}, bf16[7168,64]{0,1:T(8,128)(2,1)}, u32[]{:S(2)}) copy-start(bf16[7168,64]{0,1:T(8,128)(2,1)} %param.8) | copy-start | bytes 2752516
  3.4 0.9 %copy-start.2 = (bf16[2048,64]{0,1:T(8,128)(2,1)S(1)}, bf16[2048,64]{0,1:T(8,128)(2,1)}, u32[]{:S(2)}) copy-start(bf16[2048,64]{0,1:T(8,128)(2,1)} %param.9) | copy-start | bytes 786436
  4.4 23.7 %copy-start.3 = (bf16[64,2048]{1,0:T(8,128)(2,1)S(1)}, bf16[64,2048]{1,0:T(8,128)(2,1)}, u32[]{:S(2)}) copy-start(bf16[64,2048]{1,0:T(8,128)(2,1)} %rest_8_.1) | copy-start | bytes 786436
  17.5 6.7 %collective-permute-start = (bf16[96,1024]{1,0:T(8,128)(2,1)S(1)}, bf16[96,1024]{1,0:T(8,128)(2,1)S(1)}, u32[]{:S(2)}, u32[]{:S(2)}) collective-permute-start(bf16[96,1024]{1,0:T(8,128)(2,1)S(1)} %bitcast.14), channel_id=1, source_target_pairs={{0,2},{2,0},{1,3},{3,1},{4,6},{6,4},{5,7},{7,5},{8,10},{10,8},{9,1... | collective-permute-start | bytes 589832 | tf_op jit(solution)/shard_map/ppermute | solution.py:170
  25.5 9.6 %collective-permute-start.6 = (bf16[32,2048]{1,0:T(8,128)(2,1)S(1)}, bf16[32,2048]{1,0:T(8,128)(2,1)S(1)}, u32[]{:S(2)}, u32[]{:S(2)}) collective-permute-start(bf16[32,2048]{1,0:T(8,128)(2,1)S(1)} %features.1.rest_0_), channel_id=1, source_target_pairs={{0,12},{4,8},{8,4},{12,0},{16,28},{20,24},{24,20},{28,16},{1,13},{... | collective-permute-start | bytes 393224 | tf_op jit(solution)/shard_map/ppermute | solution.py:175
  28.1 13.5 %collective-permute-start.8 = (bf16[64,2048]{1,0:T(8,128)(2,1)S(1)}, bf16[64,2048]{1,0:T(8,128)(2,1)S(1)}, u32[]{:S(2)}, u32[]{:S(2)}) collective-permute-start(bf16[64,2048]{1,0:T(8,128)(2,1)S(1)} %copy-done.3), channel_id=1, source_target_pairs={{0,16},{4,20},{8,24},{12,28},{16,0},{20,4},{24,8},{28,12},{1,17},{... | collective-permute-start | bytes 786440 | tf_op jit(solution)/shard_map/ppermute | solution.py:166
  30.7 8.4 %collective-permute-start.4 = (bf16[32,2048]{1,0:T(8,128)(2,1)S(1)}, bf16[32,2048]{1,0:T(8,128)(2,1)S(1)}, u32[]{:S(2)}, u32[]{:S(2)}) collective-permute-start(bf16[32,2048]{1,0:T(8,128)(2,1)S(1)} %features.1.rest_0_), channel_id=1, source_target_pairs={{0,8},{4,12},{8,0},{12,4},{16,24},{20,28},{24,16},{28,20},{1,9},{5... | collective-permute-start | bytes 393224 | tf_op jit(solution)/shard_map/ppermute | solution.py:175
  31.1 7.9 %collective-permute-start.2 = (bf16[32,2048]{1,0:T(8,128)(2,1)S(1)}, bf16[32,2048]{1,0:T(8,128)(2,1)S(1)}, u32[]{:S(2)}, u32[]{:S(2)}) collective-permute-start(bf16[32,2048]{1,0:T(8,128)(2,1)S(1)} %features.1.rest_0_), channel_id=1, source_target_pairs={{0,4},{4,0},{8,12},{12,8},{16,20},{20,16},{24,28},{28,24},{1,5},{5... | collective-permute-start | bytes 393224 | tf_op jit(solution)/shard_map/ppermute | solution.py:175
  31.7 9.9 %collective-permute-start.1 = (bf16[32,2048]{1,0:T(8,128)(2,1)S(1)}, bf16[32,2048]{1,0:T(8,128)(2,1)S(1)}, u32[]{:S(2)}, u32[]{:S(2)}) collective-permute-start(bf16[32,2048]{1,0:T(8,128)(2,1)S(1)} %features.1.rest_0_), channel_id=1, source_target_pairs={{0,1},{1,0},{2,3},{3,2},{4,5},{5,4},{6,7},{7,6},{8,9},{9,8},{10,11... | collective-permute-start | bytes 393224 | tf_op jit(solution)/shard_map/ppermute | solution.py:178
  35.1 6.5 %collective-permute-start.7 = (bf16[32,2048]{1,0:T(8,128)(2,1)S(1)}, bf16[32,2048]{1,0:T(8,128)(2,1)S(1)}, u32[]{:S(2)}, u32[]{:S(2)}) collective-permute-start(bf16[32,2048]{1,0:T(8,128)(2,1)S(1)} %collective-permute-done.6.rest_6_), channel_id=1, source_target_pairs={{0,1},{1,0},{2,3},{3,2},{4,5},{5,4},{6,7},{7,6},{8,9},{9,8},{10,11... | collective-permute-start | bytes 393224 | tf_op jit(solution)/shard_map/ppermute | solution.py:178
  39.1 2.5 %collective-permute-start.5 = (bf16[32,2048]{1,0:T(8,128)(2,1)S(1)}, bf16[32,2048]{1,0:T(8,128)(2,1)S(1)}, u32[]{:S(2)}, u32[]{:S(2)}) collective-permute-start(bf16[32,2048]{1,0:T(8,128)(2,1)S(1)} %collective-permute-done.4.rest_4_), channel_id=1, source_target_pairs={{0,1},{1,0},{2,3},{3,2},{4,5},{5,4},{6,7},{7,6},{8,9},{9,8},{10,11... | collective-permute-start | bytes 393224 | tf_op jit(solution)/shard_map/ppermute | solution.py:178
  39.1 2.5 %collective-permute-start.3 = (bf16[32,2048]{1,0:T(8,128)(2,1)S(1)}, bf16[32,2048]{1,0:T(8,128)(2,1)S(1)}, u32[]{:S(2)}, u32[]{:S(2)}) collective-permute-start(bf16[32,2048]{1,0:T(8,128)(2,1)S(1)} %collective-permute-done.2.rest_2_), channel_id=1, source_target_pairs={{0,1},{1,0},{2,3},{3,2},{4,5},{5,4},{6,7},{7,6},{8,9},{9,8},{10,11... | collective-permute-start | bytes 393224 | tf_op jit(solution)/shard_map/ppermute | solution.py:178
  43.0 6.6 %collective-permute-start.10 = (f32[64,256]{1,0:T(8,128)S(1)}, f32[64,256]{1,0:T(8,128)S(1)}, u32[]{:S(2)}, u32[]{:S(2)}) collective-permute-start(f32[64,256]{1,0:T(8,128)S(1)} %get-tuple-element.12), channel_id=1, source_target_pairs={{0,16},{2,0},{4,20},{6,4},{8,24},{10,8},{12,28},{14,12},{16,18},{1... | collective-permute-start | bytes 196616 | tf_op jit(solution)/shard_map/ppermute | solution.py:184
  43.6 9.3 %collective-permute-start.9 = (f32[64,256]{1,0:T(8,128)S(1)}, f32[64,256]{1,0:T(8,128)S(1)}, u32[]{:S(2)}, u32[]{:S(2)}) collective-permute-start(f32[64,256]{1,0:T(8,128)S(1)} %get-tuple-element.11), channel_id=1, source_target_pairs={{2,16},{6,20},{10,24},{14,28},{16,2},{20,6},{24,10},{28,14},{3,17}... | collective-permute-start | bytes 196616 | tf_op jit(solution)/shard_map/ppermute | solution.py:184

commit v2 on v1

--- a/solution.py
+++ b/solution.py
@@ -13,47 +13,52 @@
 NT = (((1,), (1,)), ((), ()))
 VMEM = pl.BlockSpec(memory_space=pltpu.VMEM)
 SMEM = pl.BlockSpec(memory_space=pltpu.SMEM)
-ANY = pl.BlockSpec(memory_space=pl.ANY)
-
-
-def tiles(length, tile):
-    return [(start, min(tile, length - start)) for start in range(0, length, tile)]
-
-
-def project_kernel(parts, place, hidden, grads, w_in, w_out, keep, send, h_buf, g_buf, wi_buf, wo_buf, out_side, h_sem, g_sem, w_sem):
+HBM = pl.BlockSpec(memory_space=pltpu.HBM)
+
+
+def project_kernel(parts, tile, place, hidden, grads, w_in, w_out, keep, send, h_buf, g_buf, wi_buf, wo_buf, out_side, h_sem, g_sem, w_sem):
     length, width = h_buf.shape[0], w_in.shape[0]
-    block = width // parts
-    weights = [pltpu.make_async_copy(w_out, wo_buf, w_sem.at[0]), pltpu.make_async_copy(w_in, wi_buf, w_sem.at[1])]
-    spans = tiles(length, 256)
-    weights[0].start()
-    copies = []
-    for n, (start, size) in enumerate(spans):
-        rows = pl.ds(start, size)
-        copies.append(
-            (
-                pltpu.make_async_copy(grads.at[rows], g_buf.at[rows], g_sem.at[n]),
-                pltpu.make_async_copy(hidden.at[rows], h_buf.at[rows], h_sem.at[n]),
-            )
+    block, steps = width // parts, length // tile
+
+    def rows_of(n):
+        return pl.ds(pl.multiple_of(n * tile, tile), tile)
+
+    def copies(n):
+        rows = rows_of(n)
+        return (
+            pltpu.make_async_copy(grads.at[rows], g_buf.at[rows], g_sem.at[n]),
+            pltpu.make_async_copy(hidden.at[rows], h_buf.at[rows], h_sem.at[n]),
         )
-    copies[0][0].start()
-    weights[1].start()
-    copies[0][1].start()
-    for first, second in copies[1:]:
-        first.start()
-        second.start()
-    for n, (start, size) in enumerate(spans):
-        rows = slice(start, start + size)
-        if n == 0:
-            weights[0].wait()
-        copies[n][0].wait()
-        out_side[:, rows] = lax.dot_general(wo_buf[...], g_buf[rows], NT, preferred_element_type=jnp.float32)
-        if n == 0:
-            weights[1].wait()
-        copies[n][1].wait()
-        act = lax.dot_general(wi_buf[...], h_buf[rows], NT, preferred_element_type=jnp.float32)
-        keep[:width, rows] = act
+
+    weights = (pltpu.make_async_copy(w_out, wo_buf, w_sem.at[0]), pltpu.make_async_copy(w_in, wi_buf, w_sem.at[1]))
+    for weight, copy in zip(weights, copies(0)):
+        weight.start()
+        copy.start()
+    for copy in copies(1) if steps > 1 else ():
+        copy.start()
+    for weight in weights:
+        weight.wait()
+
+    def step(n, carry):
+        rows = rows_of(n)
+        for copy in copies(n):
+            copy.wait()
+
+        @pl.when(n + 2 < steps)
+        def _():
+            for copy in copies(n + 2):
+                copy.start()
+
+        act = lax.dot_general(h_buf[rows], wi_buf[...], NT, preferred_element_type=jnp.float32)
+        side = lax.dot_general(g_buf[rows], wo_buf[...], NT, preferred_element_type=jnp.float32)
+        both = jnp.concatenate([act, side], axis=1).T
+        keep[:width, rows] = both[:width]
         for d in range(1, parts):
-            send[d - 1, :width, rows] = act.astype(jnp.bfloat16)
+            send[d - 1, :width, rows] = both[:width].astype(jnp.bfloat16)
+        out_side[:, rows] = both[width:]
+        return carry
+
+    lax.fori_loop(0, steps, step, 0)
     keep[width:] = out_side[pl.ds(pl.multiple_of(place[0] * block, block), block)]
     for d in range(1, parts):
         there = lax.rem(place[0] + d, parts)
@@ -62,14 +67,15 @@
 
 def project(parts, place, hidden, grads, w_in, w_out):
     (length, units), features, width = hidden.shape, grads.shape[1], w_in.shape[0]
-    rows, steps = width + width // parts, len(tiles(length, 256))
+    tile = math.gcd(length, 256)
+    rows, steps = width + width // parts, length // tile
     return pl.pallas_call(
-        functools.partial(project_kernel, parts),
+        functools.partial(project_kernel, parts, tile),
         out_shape=(
             jax.ShapeDtypeStruct((rows, length), jnp.float32),
             jax.ShapeDtypeStruct((max(parts - 1, 1), rows, length), jnp.bfloat16),
         ),
-        in_specs=[SMEM, ANY, ANY, ANY, ANY],
+        in_specs=[SMEM, HBM, HBM, HBM, HBM],
         out_specs=(VMEM, VMEM),
         scratch_shapes=[
             pltpu.VMEM((length, units), jnp.bfloat16),
@@ -83,7 +89,7 @@
         ],
         compiler_params=pltpu.CompilerParams(vmem_limit_bytes=40 * MIB),
         name="project",
-    )(place, hidden, grads, w_in, w_out)
+    )(place, *(pltpu.with_memory_space_constraint(a, pltpu.HBM) for a in (hidden, grads, w_in, w_out)))
 
 
 def features_kernel(width, segment, keep, *rest):
@@ -178,7 +184,7 @@
             blocks.append(lax.ppermute(block, "dp", pairs) if e else block)
     partial = scores(parts, members, cores, place, blocks, asked)
     total = None
-    for k in range(parts):
+    for k in reversed(range(parts)):
         routes = [(a * members + m, b, (b + k) % parts * members + m, a) for a in around for m in range(members) for b in around]
         pairs = [(s * parts + b, t * parts + a) for s, b, t, a in routes if (s, b) != (t, a)]
         arrived = lax.ppermute(partial[k], ("query", "tensor"), pairs)
@@ -198,5 +204,6 @@
         P(("query", "dp"), "tensor"),
     )
     out_specs = P("tensor", ("query", "dp"))
-    step = functools.partial(local, mesh.shape["query"], mesh.shape["tensor"], mesh.shape["dp"])
-    return jax.shard_map(step, mesh=mesh, in_specs=in_specs, out_specs=out_specs, check_vma=False)
+    body = functools.partial(local, mesh.shape["query"], mesh.shape["tensor"], mesh.shape["dp"])
+
+    return jax.shard_map(body, mesh=mesh, in_specs=in_specs, out_specs=out_specs, check_vma=False)

time: 53.8 us -> 45.6 us (0.85)
  local copies, waits for them, and re-layouts: 4.32 us -> 0.01 us
  Pallas kernels: 15.8 us -> 12 us
    unnamed x10 -> x4, local copies, waits for them, and re-layouts: 4.32 us -> 0.01 us
    pallas_call x1, Pallas kernels: 13.1 us -> 9.32 us  [project(): pl.pallas_call(functools.partial(project_kernel, parts, tile), out_shape=...]
where the time goes in v2:
time: 45.6 us; the launch traced here: 45.5 us
  waiting for transfers between devices  20.7 us (45%)
  Pallas kernels  12 us (26%)
  starting transfers between devices  12 us (26%)
  other arithmetic  0.72 us (2%)
    pallas_call x1, Pallas kernels, project(): pl.pallas_call(functools.partial(project_kernel, parts, tile), out_shape=...  9.32 us
    ppermute x3, waiting for transfers between devices, local(): block = lax.ppermute(own, 'query', pairs) if d else own  7.37 us
    ppermute x1, waiting for transfers between devices, local(): lax.ppermute(send[d - 1], 'tensor', [(a, (a + d) % parts) for a in around])  6.63 us
    ppermute x2, starting transfers between devices, local(): arrived = lax.ppermute(partial[k], ('query', 'tensor'), pairs)  5.27 us
    ppermute x2, waiting for transfers between devices, local(): arrived = lax.ppermute(partial[k], ('query', 'tensor'), pairs)  4.63 us
    ppermute x3, starting transfers between devices, local(): block = lax.ppermute(own, 'query', pairs) if d else own  3.52 us
    ppermute x1, starting transfers between devices, local(): asked.append(lax.ppermute(queries, 'query', pairs))  2.58 us
    ppermute x1, waiting for transfers between devices, local(): asked.append(lax.ppermute(queries, 'query', pairs))  2.05 us
  transfers between devices with their start and end apart: 11, of which 6 were waited for; matrix products, arithmetic and copies ran while one was open for 0% of the time, Pallas kernels for 0%

profile of v2, /device:TPU:2, one launch (start us, length us, event | category | flops | bytes accessed | tf_op | source)
XLA Modules:
  0.0 45.5 jit_solution(3781502897815603171)
XLA Ops:
  0.0 0.0 copy-start.1
  0.0 0.0 copy-start
  0.0 0.1 pad_add_fusion.place
  0.1 9.3 %project.1 = (f32[96,1024]{1,0:T(8,128)S(1)}, bf16[1,96,1024]{2,1,0:T(8,128)(2,1)S(1)}) custom-call(s32[4]{0:T(128)S(1)} %pad_add_fusion.place, bf16[1024,7168]{1,0:T(8,128)(2,1)} %bitcast.12, bf16[1024,2048]{1,0:T(8,128)(2,1)} %bitcast.13, bf16[64,7168]{1,0:T(8,128)(2,1)} %bitcast.14, bf16[64,2048]{1,0:T(8,128)(2,1)} %bitcast.15), custom_call_target="tpu_custom_call" | custom-call | tf_op jit(solution)/shard_map/project/pallas_call | solution.py:72
  9.4 0.1 collective-permute-start
  9.5 6.6 %collective-permute-done.rest_0_ = bf16[96,1024]{1,0:T(8,128)(2,1)S(1)} collective-permute-done((bf16[96,1024]{1,0:T(8,128)(2,1)S(1)}, bf16[96,1024]{1,0:T(8,128)(2,1)S(1)}, u32[]{:S(2)}, u32[]{:S(2)}) %collective-permute-start) | collective-permute-done | bytes 196640 | tf_op jit(solution)/shard_map/ppermute | solution.py:176
  16.1 0.0 copy-done.1
  16.1 1.3 %features.1.rest_0_ = bf16[32,2048]{1,0:T(8,128)(2,1)S(1)} custom-call(s32[1,1024]{1,0:T(1,128)S(1)} %copy-done.1, f32[96,1024]{1,0:T(8,128)S(1)} %get-tuple-element.9.keep, bf16[96,1024]{1,0:T(8,128)(2,1)S(1)} %collective-permute-done.rest_0_), custom_call_target="tpu_custom_call" | custom-call | tf_op jit(solution)/shard_map/features/pallas_call | solution.py:113
  17.5 2.6 %collective-permute-start.6 = (bf16[32,2048]{1,0:T(8,128)(2,1)S(1)}, bf16[32,2048]{1,0:T(8,128)(2,1)S(1)}, u32[]{:S(2)}, u32[]{:S(2)}) collective-permute-start(bf16[32,2048]{1,0:T(8,128)(2,1)S(1)} %features.1.rest_0_), channel_id=1, source_target_pairs={{0,12},{4,8},{8,4},{12,0},{16,28},{20,24},{24,20},{28,16},{1,13},{... | collective-permute-start | bytes 393224 | tf_op jit(solution)/shard_map/ppermute | solution.py:181
  20.0 0.0 copy-done
  20.0 2.6 %collective-permute-start.8 = (bf16[64,2048]{1,0:T(8,128)(2,1)S(1)}, bf16[64,2048]{1,0:T(8,128)(2,1)S(1)}, u32[]{:S(2)}, u32[]{:S(2)}) collective-permute-start(bf16[64,2048]{1,0:T(8,128)(2,1)S(1)} %copy-done), channel_id=1, source_target_pairs={{0,16},{4,20},{8,24},{12,28},{16,0},{20,4},{24,8},{28,12},{1,17},{... | collective-permute-start | bytes 786440 | tf_op jit(solution)/shard_map/ppermute | solution.py:172
  22.6 0.5 %collective-permute-start.4 = (bf16[32,2048]{1,0:T(8,128)(2,1)S(1)}, bf16[32,2048]{1,0:T(8,128)(2,1)S(1)}, u32[]{:S(2)}, u32[]{:S(2)}) collective-permute-start(bf16[32,2048]{1,0:T(8,128)(2,1)S(1)} %features.1.rest_0_), channel_id=1, source_target_pairs={{0,8},{4,12},{8,0},{12,4},{16,24},{20,28},{24,16},{28,20},{1,9},{5... | collective-permute-start | bytes 393224 | tf_op jit(solution)/shard_map/ppermute | solution.py:181
  23.1 0.5 %collective-permute-start.2 = (bf16[32,2048]{1,0:T(8,128)(2,1)S(1)}, bf16[32,2048]{1,0:T(8,128)(2,1)S(1)}, u32[]{:S(2)}, u32[]{:S(2)}) collective-permute-start(bf16[32,2048]{1,0:T(8,128)(2,1)S(1)} %features.1.rest_0_), channel_id=1, source_target_pairs={{0,4},{4,0},{8,12},{12,8},{16,20},{20,16},{24,28},{28,24},{1,5},{5... | collective-permute-start | bytes 393224 | tf_op jit(solution)/shard_map/ppermute | solution.py:181
  23.6 0.0 collective-permute-start.1
  23.6 3.4 %collective-permute-done.6.rest_6_ = bf16[32,2048]{1,0:T(8,128)(2,1)S(1)} collective-permute-done((bf16[32,2048]{1,0:T(8,128)(2,1)S(1)}, bf16[32,2048]{1,0:T(8,128)(2,1)S(1)}, u32[]{:S(2)}, u32[]{:S(2)}) %collective-permute-start.6) | collective-permute-done | bytes 131104 | tf_op jit(solution)/shard_map/ppermute | solution.py:181
  27.0 0.0 collective-permute-start.7
  27.0 3.9 %collective-permute-done.4.rest_4_ = bf16[32,2048]{1,0:T(8,128)(2,1)S(1)} collective-permute-done((bf16[32,2048]{1,0:T(8,128)(2,1)S(1)}, bf16[32,2048]{1,0:T(8,128)(2,1)S(1)}, u32[]{:S(2)}, u32[]{:S(2)}) %collective-permute-start.4) | collective-permute-done | bytes 131104 | tf_op jit(solution)/shard_map/ppermute | solution.py:181
  30.9 0.0 collective-permute-start.5
  30.9 0.0 collective-permute-done.2.rest_2_
  30.9 0.5 %collective-permute-start.3 = (bf16[32,2048]{1,0:T(8,128)(2,1)S(1)}, bf16[32,2048]{1,0:T(8,128)(2,1)S(1)}, u32[]{:S(2)}, u32[]{:S(2)}) collective-permute-start(bf16[32,2048]{1,0:T(8,128)(2,1)S(1)} %collective-permute-done.2.rest_2_), channel_id=1, source_target_pairs={{0,1},{1,0},{2,3},{3,2},{4,5},{5,4},{6,7},{7,6},{8,9},{9,8},{10,11... | collective-permute-start | bytes 393224 | tf_op jit(solution)/shard_map/ppermute | solution.py:184
  31.5 2.0 %collective-permute-done.8.rest_9_ = bf16[64,2048]{1,0:T(8,128)(2,1)S(1)} collective-permute-done((bf16[64,2048]{1,0:T(8,128)(2,1)S(1)}, bf16[64,2048]{1,0:T(8,128)(2,1)S(1)}, u32[]{:S(2)}, u32[]{:S(2)}) %collective-permute-start.8) | collective-permute-done | bytes 262176 | tf_op jit(solution)/shard_map/ppermute | solution.py:172
  33.5 0.0 collective-permute-done.1.rest_1_
  33.5 0.0 collective-permute-done.7.rest_7_
  33.5 0.0 collective-permute-done.5.rest_5_
  33.5 0.0 collective-permute-done.3.rest_3_
  33.5 1.4 %scores.1 = (f32[64,256]{1,0:T(8,128)S(1)}, f32[64,256]{1,0:T(8,128)S(1)}) custom-call(s32[4]{0:T(128)S(1)} %pad_add_fusion.place, bf16[32,2048]{1,0:T(8,128)(2,1)S(1)} %features.1.rest_0_, bf16[32,2048]{1,0:T(8,128)(2,1)S(1)} %collective-permute-done.1.rest_1_, bf16[32,2048]{1,0:T(8,128)(2,1)S(1)} %collective-permute-done.2.rest_2_, ...), custom_call_target="tpu_custom_call" | custom-call | tf_op jit(solution)/shard_map/scores/pallas_call | solution.py:143
  34.9 0.6 %collective-permute-start.9 = (f32[64,256]{1,0:T(8,128)S(1)}, f32[64,256]{1,0:T(8,128)S(1)}, u32[]{:S(2)}, u32[]{:S(2)}) collective-permute-start(f32[64,256]{1,0:T(8,128)S(1)} %get-tuple-element.11), channel_id=1, source_target_pairs={{0,16},{2,0},{4,20},{6,4},{8,24},{10,8},{12,28},{14,12},{16,18},{1... | collective-permute-start | bytes 196616 | tf_op jit(solution)/shard_map/ppermute | solution.py:190
  35.5 4.7 %collective-permute-start.10 = (f32[64,256]{1,0:T(8,128)S(1)}, f32[64,256]{1,0:T(8,128)S(1)}, u32[]{:S(2)}, u32[]{:S(2)}) collective-permute-start(f32[64,256]{1,0:T(8,128)S(1)} %get-tuple-element.12), channel_id=1, source_target_pairs={{2,16},{6,20},{10,24},{14,28},{16,2},{20,6},{24,10},{28,14},{3,17}... | collective-permute-start | bytes 196616 | tf_op jit(solution)/shard_map/ppermute | solution.py:190
  40.2 1.3 %collective-permute-done.9 = f32[64,256]{1,0:T(8,128)S(1)} collective-permute-done((f32[64,256]{1,0:T(8,128)S(1)}, f32[64,256]{1,0:T(8,128)S(1)}, u32[]{:S(2)}, u32[]{:S(2)}) %collective-permute-start.9) | collective-permute-done | bytes 65568 | tf_op jit(solution)/shard_map/ppermute | solution.py:190
  41.5 3.3 %collective-permute-done.10 = f32[64,256]{1,0:T(8,128)S(1)} collective-permute-done((f32[64,256]{1,0:T(8,128)S(1)}, f32[64,256]{1,0:T(8,128)S(1)}, u32[]{:S(2)}, u32[]{:S(2)}) %collective-permute-start.10) | collective-permute-done | bytes 65568 | tf_op jit(solution)/shard_map/ppermute | solution.py:190
  44.8 0.6 %add_bitcast_fusion = f32[256,64]{0,1:T(8,128)} fusion(f32[64,256]{1,0:T(8,128)S(1)} %collective-permute-done.9, f32[64,256]{1,0:T(8,128)S(1)} %get-tuple-element.12, f32[64,256]{1,0:T(8,128)S(1)} %collective-permute-done.10, pred[]{:T(512)S(6)} %and.13), kind=kLoop, calls=%fused_computation | loop fusion | flops 32768 | bytes 262145 | tf_op jit(solution)/shard_map/transpose | solution.py:194
Async XLA Ops:
  0.0 16.1 %copy-start.1 = (s32[1,1024]{1,0:T(1,128)S(1)}, s32[1,1024]{1,0:T(1,128)}, u32[]{:S(2)}) copy-start(s32[1,1024]{1,0:T(1,128)} %segment.1) | copy-start | bytes 12292
  0.0 20.0 %copy-start = (bf16[64,2048]{1,0:T(8,128)(2,1)S(1)}, bf16[64,2048]{1,0:T(8,128)(2,1)}, u32[]{:S(2)}) copy-start(bf16[64,2048]{1,0:T(8,128)(2,1)} %rest_8_.1) | copy-start | bytes 786436
  9.4 6.7 %collective-permute-start = (bf16[96,1024]{1,0:T(8,128)(2,1)S(1)}, bf16[96,1024]{1,0:T(8,128)(2,1)S(1)}, u32[]{:S(2)}, u32[]{:S(2)}) collective-permute-start(bf16[96,1024]{1,0:T(8,128)(2,1)S(1)} %bitcast.11), channel_id=1, source_target_pairs={{0,2},{2,0},{1,3},{3,1},{4,6},{6,4},{5,7},{7,5},{8,10},{10,8},{9,1... | collective-permute-start | bytes 589832 | tf_op jit(solution)/shard_map/ppermute | solution.py:176
  17.5 9.5 %collective-permute-start.6 = (bf16[32,2048]{1,0:T(8,128)(2,1)S(1)}, bf16[32,2048]{1,0:T(8,128)(2,1)S(1)}, u32[]{:S(2)}, u32[]{:S(2)}) collective-permute-start(bf16[32,2048]{1,0:T(8,128)(2,1)S(1)} %features.1.rest_0_), channel_id=1, source_target_pairs={{0,12},{4,8},{8,4},{12,0},{16,28},{20,24},{24,20},{28,16},{1,13},{... | collective-permute-start | bytes 393224 | tf_op jit(solution)/shard_map/ppermute | solution.py:181
  20.0 13.5 %collective-permute-start.8 = (bf16[64,2048]{1,0:T(8,128)(2,1)S(1)}, bf16[64,2048]{1,0:T(8,128)(2,1)S(1)}, u32[]{:S(2)}, u32[]{:S(2)}) collective-permute-start(bf16[64,2048]{1,0:T(8,128)(2,1)S(1)} %copy-done), channel_id=1, source_target_pairs={{0,16},{4,20},{8,24},{12,28},{16,0},{20,4},{24,8},{28,12},{1,17},{... | collective-permute-start | bytes 786440 | tf_op jit(solution)/shard_map/ppermute | solution.py:172
  22.6 8.3 %collective-permute-start.4 = (bf16[32,2048]{1,0:T(8,128)(2,1)S(1)}, bf16[32,2048]{1,0:T(8,128)(2,1)S(1)}, u32[]{:S(2)}, u32[]{:S(2)}) collective-permute-start(bf16[32,2048]{1,0:T(8,128)(2,1)S(1)} %features.1.rest_0_), channel_id=1, source_target_pairs={{0,8},{4,12},{8,0},{12,4},{16,24},{20,28},{24,16},{28,20},{1,9},{5... | collective-permute-start | bytes 393224 | tf_op jit(solution)/shard_map/ppermute | solution.py:181
  23.1 7.9 %collective-permute-start.2 = (bf16[32,2048]{1,0:T(8,128)(2,1)S(1)}, bf16[32,2048]{1,0:T(8,128)(2,1)S(1)}, u32[]{:S(2)}, u32[]{:S(2)}) collective-permute-start(bf16[32,2048]{1,0:T(8,128)(2,1)S(1)} %features.1.rest_0_), channel_id=1, source_target_pairs={{0,4},{4,0},{8,12},{12,8},{16,20},{20,16},{24,28},{28,24},{1,5},{5... | collective-permute-start | bytes 393224 | tf_op jit(solution)/shard_map/ppermute | solution.py:181
  23.6 9.9 %collective-permute-start.1 = (bf16[32,2048]{1,0:T(8,128)(2,1)S(1)}, bf16[32,2048]{1,0:T(8,128)(2,1)S(1)}, u32[]{:S(2)}, u32[]{:S(2)}) collective-permute-start(bf16[32,2048]{1,0:T(8,128)(2,1)S(1)} %features.1.rest_0_), channel_id=1, source_target_pairs={{0,1},{1,0},{2,3},{3,2},{4,5},{5,4},{6,7},{7,6},{8,9},{9,8},{10,11... | collective-permute-start | bytes 393224 | tf_op jit(solution)/shard_map/ppermute | solution.py:184
  27.0 6.5 %collective-permute-start.7 = (bf16[32,2048]{1,0:T(8,128)(2,1)S(1)}, bf16[32,2048]{1,0:T(8,128)(2,1)S(1)}, u32[]{:S(2)}, u32[]{:S(2)}) collective-permute-start(bf16[32,2048]{1,0:T(8,128)(2,1)S(1)} %collective-permute-done.6.rest_6_), channel_id=1, source_target_pairs={{0,1},{1,0},{2,3},{3,2},{4,5},{5,4},{6,7},{7,6},{8,9},{9,8},{10,11... | collective-permute-start | bytes 393224 | tf_op jit(solution)/shard_map/ppermute | solution.py:184
  30.9 2.6 %collective-permute-start.5 = (bf16[32,2048]{1,0:T(8,128)(2,1)S(1)}, bf16[32,2048]{1,0:T(8,128)(2,1)S(1)}, u32[]{:S(2)}, u32[]{:S(2)}) collective-permute-start(bf16[32,2048]{1,0:T(8,128)(2,1)S(1)} %collective-permute-done.4.rest_4_), channel_id=1, source_target_pairs={{0,1},{1,0},{2,3},{3,2},{4,5},{5,4},{6,7},{7,6},{8,9},{9,8},{10,11... | collective-permute-start | bytes 393224 | tf_op jit(solution)/shard_map/ppermute | solution.py:184
  30.9 2.6 %collective-permute-start.3 = (bf16[32,2048]{1,0:T(8,128)(2,1)S(1)}, bf16[32,2048]{1,0:T(8,128)(2,1)S(1)}, u32[]{:S(2)}, u32[]{:S(2)}) collective-permute-start(bf16[32,2048]{1,0:T(8,128)(2,1)S(1)} %collective-permute-done.2.rest_2_), channel_id=1, source_target_pairs={{0,1},{1,0},{2,3},{3,2},{4,5},{5,4},{6,7},{7,6},{8,9},{9,8},{10,11... | collective-permute-start | bytes 393224 | tf_op jit(solution)/shard_map/ppermute | solution.py:184
  34.9 6.6 %collective-permute-start.9 = (f32[64,256]{1,0:T(8,128)S(1)}, f32[64,256]{1,0:T(8,128)S(1)}, u32[]{:S(2)}, u32[]{:S(2)}) collective-permute-start(f32[64,256]{1,0:T(8,128)S(1)} %get-tuple-element.11), channel_id=1, source_target_pairs={{0,16},{2,0},{4,20},{6,4},{8,24},{10,8},{12,28},{14,12},{16,18},{1... | collective-permute-start | bytes 196616 | tf_op jit(solution)/shard_map/ppermute | solution.py:190
  35.5 9.3 %collective-permute-start.10 = (f32[64,256]{1,0:T(8,128)S(1)}, f32[64,256]{1,0:T(8,128)S(1)}, u32[]{:S(2)}, u32[]{:S(2)}) collective-permute-start(f32[64,256]{1,0:T(8,128)S(1)} %get-tuple-element.12), channel_id=1, source_target_pairs={{2,16},{6,20},{10,24},{14,28},{16,2},{20,6},{24,10},{28,14},{3,17}... | collective-permute-start | bytes 196616 | tf_op jit(solution)/shard_map/ppermute | solution.py:190

commit v3 on v2

--- a/solution.py
+++ b/solution.py
@@ -120,32 +120,35 @@
     )(segment, keep, *received)
 
 
-def scores_kernel(parts, members, cores, place, *rest):
-    count = members * cores
-    blocks, queries = rest[:count], rest[count : count + parts]
-    outs, table = rest[count + parts : count + 2 * parts], rest[-1]
-    x, h, g, core = place[0], place[1], place[2], place[3]
-    for d in range(members):
+def scores_kernel(parts, near, cores, place, *rest):
+    count = near * cores
+    blocks, rest = rest[:count], rest[count:]
+    asked = len(rest) // 2 - 1
+    queries, outs, docs, rows = rest[:asked], rest[asked : 2 * asked], rest[-2], rest[-1]
+    x, h, b, core = place[0], place[1], place[2], place[3]
+    far, own = asked // parts, queries[0].shape[0]
+    for d in range(parts):
+        k = lax.rem(h - x - d + 2 * parts, parts)
+        for s in range(far):
+            rows[pl.ds(pl.multiple_of((k * far + s) * own, own), own)] = queries[d * far + s][...]
+    for d in range(near):
         for e in range(cores):
-            at = holds(g, d, members) * cores + holds(core, e, cores)
-            table[pl.ds(pl.multiple_of(at * SEGS, SEGS), SEGS)] = blocks[d * cores + e][...]
-    for k in range(parts):
-        which = lax.rem(h - x - k + 2 * parts, parts)
-        chosen = queries[0][...]
-        for d in range(1, parts):
-            chosen = jnp.where(which == d, queries[d][...], chosen)
-        outs[k][...] = lax.dot_general(chosen, table[...], NT, preferred_element_type=jnp.float32)
-
-
-def scores(parts, members, cores, place, blocks, queries):
+            at = holds(b, d, near) * cores + holds(core, e, cores)
+            docs[pl.ds(pl.multiple_of(at * SEGS, SEGS), SEGS)] = blocks[d * cores + e][...]
+    table = lax.dot_general(rows[...], docs[...], NT, preferred_element_type=jnp.float32)
+    for n, out in enumerate(outs):
+        out[...] = table[n * own : (n + 1) * own]
+
+
+def scores(parts, near, cores, place, blocks, queries):
     docs, width = SEGS * len(blocks), blocks[0].shape[1]
     own = queries[0].shape[0]
     return pl.pallas_call(
-        functools.partial(scores_kernel, parts, members, cores),
-        out_shape=(jax.ShapeDtypeStruct((own, docs), jnp.float32),) * parts,
-        in_specs=[SMEM] + [VMEM] * (len(blocks) + parts),
-        out_specs=(VMEM,) * parts,
-        scratch_shapes=[pltpu.VMEM((docs, width), jnp.bfloat16)],
+        functools.partial(scores_kernel, parts, near, cores),
+        out_shape=(jax.ShapeDtypeStruct((own, docs), jnp.float32),) * len(queries),
+        in_specs=[SMEM] + [VMEM] * (len(blocks) + len(queries)),
+        out_specs=(VMEM,) * len(queries),
+        scratch_shapes=[pltpu.VMEM((docs, width), jnp.bfloat16), pltpu.VMEM((own * len(queries), width), jnp.bfloat16)],
         compiler_params=pltpu.CompilerParams(vmem_limit_bytes=40 * MIB),
         name="scores",
     )(place, *blocks, *queries)
@@ -156,42 +159,63 @@
 
 
 def holds(i, d, size):
-    return i ^ d if size & (size - 1) == 0 else lax.rem(i - d + size, size)
+    return i ^ d if size & (size - 1) == 0 else (i - d) % size
 
 
 def local(rows_axis, parts, cores, hidden, out_grad, proj_in, proj_out, seg_ids, queries):
     members = rows_axis // parts
+    near = max(n for n in range(1, math.isqrt(members) + 1) if members % n == 0)
+    far = members // near
     x, q, core = lax.axis_index("tensor"), lax.axis_index("query"), lax.axis_index("dp")
-    h, g = q // members, lax.rem(q, members)
-    place = jnp.stack([x, h, g, core]).astype(jnp.int32)
+    h, a, b = q // members, lax.rem(q, members) // near, lax.rem(q, near)
+    place = jnp.stack([x, h, b, core]).astype(jnp.int32)
     width = proj_in.shape[1]
-    around = range(parts)
-    asked = [queries]
+    every = [(i, j, m) for i in range(parts) for j in range(far) for m in range(near)]
+
+    def index(i, j, m):
+        return (i * far + j) * near + m
+
+    asked = {(0, 0): queries}
     for d in range(1, parts):
-        pairs = [(a * members + m, (a + d) % parts * members + m) for a in around for m in range(members)]
-        asked.append(lax.ppermute(queries, "query", pairs))
+        asked[d, 0] = lax.ppermute(queries, "query", [(index(i, j, m), index((i + d) % parts, j, m)) for i, j, m in every])
+    for d in range(parts):
+        for s in range(1, far):
+            asked[d, s] = lax.ppermute(asked[d, 0], "query", [(index(i, j, m), index(i, sends_to(j, s, far), m)) for i, j, m in every])
     keep, send = project(parts, place, hidden[0], out_grad[0], proj_in.T, proj_out.T)
     received = []
     for d in range(1, parts):
-        received.append(lax.ppermute(send[d - 1], "tensor", [(a, (a + d) % parts) for a in around]))
+        received.append(lax.ppermute(send[d - 1], "tensor", [(i, (i + d) % parts) for i in range(parts)]))
     own = features(width, seg_ids, keep, received)
     blocks = []
-    for d in range(members):
-        pairs = [(a * members + m, a * members + sends_to(m, d, members)) for a in around for m in range(members)]
+    for d in range(near):
+        pairs = [(index(i, j, m), index(i, j, sends_to(m, d, near))) for i, j, m in every]
         block = lax.ppermute(own, "query", pairs) if d else own
         for e in range(cores):
-            pairs = [(c, sends_to(c, e, cores)) for c in range(cores)]
-            blocks.append(lax.ppermute(block, "dp", pairs) if e else block)
-    partial = scores(parts, members, cores, place, blocks, asked)
-    total = None
-    for k in reversed(range(parts)):
-        routes = [(a * members + m, b, (b + k) % parts * members + m, a) for a in around for m in range(members) for b in around]
-        pairs = [(s * parts + b, t * parts + a) for s, b, t, a in routes if (s, b) != (t, a)]
-        arrived = lax.ppermute(partial[k], ("query", "tensor"), pairs)
-        at_home = (x == h) & (lax.rem(x + k, parts) == h)
-        arrived = jnp.where(at_home, partial[k], arrived) if len(pairs) < len(routes) else arrived
-        total = arrived if total is None else total + arrived
-    return total.T
+            blocks.append(lax.ppermute(block, "dp", [(c, sends_to(c, e, cores)) for c in range(cores)]) if e else block)
+    slots = [(k, s) for k in range(parts) for s in range(far)]
+    partial = dict(zip(slots, scores(parts, near, cores, place, blocks, [asked[slot] for slot in slots])))
+    totals = []
+    for s in range(far):
+        total = None
+        for k in range(parts):
+            routes = [
+                (index(i, j, m) * parts + t, index((t + k) % parts, int(holds(j, s, far)), m) * parts + i)
+                for i, j, m in every
+                for t in range(parts)
+            ]
+            pairs = [(source, target) for source, target in routes if source != target]
+            arrived = lax.ppermute(partial[k, s], ("query", "tensor"), pairs)
+            if len(pairs) < len(routes):
+                arrived = jnp.where((x == h) & (lax.rem(x + k, parts) == h), partial[k, s], arrived)
+            total = arrived if total is None else total + arrived
+        totals.append(total)
+    found = []
+    for j in range(far):
+        block = totals[0]
+        for s in range(1, far):
+            block = jnp.where(sends_to(a, s, far) == j, totals[s], block)
+        found.append(block)
+    return jnp.concatenate(found, axis=1).T
 
 
 def solution(mesh):

time: 45.6 us -> 41 us (0.90)
  the two profiles are of different devices: /device:TPU:2 before, /device:TPU:24 now
where the time goes in v3:
time: 41 us; the launch traced here: 40.9 us
  waiting for transfers between devices  16.2 us (40%)
  starting transfers between devices  12.1 us (30%)
  Pallas kernels  11.8 us (29%)
  other arithmetic  0.74 us (2%)
    pallas_call x1, Pallas kernels, project(): pl.pallas_call(functools.partial(project_kernel, parts, tile), out_shape=...  9.32 us
    ppermute x4, starting transfers between devices, local(): arrived = lax.ppermute(partial[k, s], ('query', 'tensor'), pairs)  7.8 us
    ppermute x4, waiting for transfers between devices, local(): arrived = lax.ppermute(partial[k, s], ('query', 'tensor'), pairs)  5.37 us
    ppermute x1, waiting for transfers between devices, local(): lax.ppermute(send[d - 1], 'tensor', [(i, (i + d) % parts) for i in range(...  4.42 us
    ppermute x1, waiting for transfers between devices, local(): block = lax.ppermute(own, 'query', pairs) if d else own  2.99 us
    ppermute x2, waiting for transfers between devices, local(): lax.ppermute(asked[d, 0], 'query', [(index(i, j, m), index(i, sends_to(j,...  2.03 us
    ppermute x1, starting transfers between devices, local(): lax.ppermute(send[d - 1], 'tensor', [(i, (i + d) % parts) for i in range(...  1.55 us
    ppermute x1, starting transfers between devices, local(): block = lax.ppermute(own, 'query', pairs) if d else own  1.55 us
  transfers between devices with their start and end apart: 11, of which 7 were waited for; matrix products, arithmetic and copies ran while one was open for 0% of the time, Pallas kernels for 26%

profile of v3, /device:TPU:24, one launch (start us, length us, event | category | flops | bytes accessed | tf_op | source)
XLA Modules:
  0.0 40.9 jit_solution(10647261657222118661)
XLA Ops:
  0.0 0.0 copy-start
  0.0 0.0 copy-start.1
  0.0 0.3 collective-permute-start.5
  0.3 0.1 pad_add_fusion.place
  0.4 9.3 %project.1 = (f32[96,1024]{1,0:T(8,128)S(1)}, bf16[1,96,1024]{2,1,0:T(8,128)(2,1)S(1)}) custom-call(s32[4]{0:T(128)S(1)} %pad_add_fusion.place, bf16[1024,7168]{1,0:T(8,128)(2,1)} %bitcast.12, bf16[1024,2048]{1,0:T(8,128)(2,1)} %bitcast.13, bf16[64,7168]{1,0:T(8,128)(2,1)} %bitcast.14, bf16[64,2048]{1,0:T(8,128)(2,1)} %bitcast.15), custom_call_target="tpu_custom_call" | custom-call | tf_op jit(solution)/shard_map/project/pallas_call | solution.py:72
  9.7 1.6 %collective-permute-start = (bf16[96,1024]{1,0:T(8,128)(2,1)S(1)}, bf16[96,1024]{1,0:T(8,128)(2,1)S(1)}, u32[]{:S(2)}, u32[]{:S(2)}) collective-permute-start(bf16[96,1024]{1,0:T(8,128)(2,1)S(1)} %bitcast.11), channel_id=1, source_target_pairs={{0,2},{2,0},{1,3},{3,1},{4,6},{6,4},{5,7},{7,5},{8,10},{10,8},{9,1... | collective-permute-start | bytes 589832 | tf_op jit(solution)/shard_map/ppermute | solution.py:187
  11.3 0.0 copy-done
  11.3 0.5 %collective-permute-start.4 = (bf16[64,2048]{1,0:T(8,128)(2,1)S(1)}, bf16[64,2048]{1,0:T(8,128)(2,1)S(1)}, u32[]{:S(2)}, u32[]{:S(2)}) collective-permute-start(bf16[64,2048]{1,0:T(8,128)(2,1)S(1)} %copy-done), channel_id=1, source_target_pairs={{0,8},{4,12},{8,0},{12,4},{16,24},{20,28},{24,16},{28,20},{1,9},{5... | collective-permute-start | bytes 786440 | tf_op jit(solution)/shard_map/ppermute | solution.py:183
  11.8 4.4 %collective-permute-done.rest_0_ = bf16[96,1024]{1,0:T(8,128)(2,1)S(1)} collective-permute-done((bf16[96,1024]{1,0:T(8,128)(2,1)S(1)}, bf16[96,1024]{1,0:T(8,128)(2,1)S(1)}, u32[]{:S(2)}, u32[]{:S(2)}) %collective-permute-start) | collective-permute-done | bytes 196640 | tf_op jit(solution)/shard_map/ppermute | solution.py:187
  16.2 0.0 copy-done.1
  16.2 1.3 %features.1.rest_0_ = bf16[32,2048]{1,0:T(8,128)(2,1)S(1)} custom-call(s32[1,1024]{1,0:T(1,128)S(1)} %copy-done.1, f32[96,1024]{1,0:T(8,128)S(1)} %get-tuple-element.11.keep, bf16[96,1024]{1,0:T(8,128)(2,1)S(1)} %collective-permute-done.rest_0_), custom_call_target="tpu_custom_call" | custom-call | tf_op jit(solution)/shard_map/features/pallas_call | solution.py:113
  17.5 1.5 %collective-permute-start.2 = (bf16[32,2048]{1,0:T(8,128)(2,1)S(1)}, bf16[32,2048]{1,0:T(8,128)(2,1)S(1)}, u32[]{:S(2)}, u32[]{:S(2)}) collective-permute-start(bf16[32,2048]{1,0:T(8,128)(2,1)S(1)} %features.1.rest_0_), channel_id=1, source_target_pairs={{0,4},{4,0},{8,12},{12,8},{16,20},{20,16},{24,28},{28,24},{1,5},{5... | collective-permute-start | bytes 393224 | tf_op jit(solution)/shard_map/ppermute | solution.py:192
  19.1 0.0 collective-permute-done.5.rest_6_
  19.1 0.4 %collective-permute-start.6 = (bf16[64,2048]{1,0:T(8,128)(2,1)S(1)}, bf16[64,2048]{1,0:T(8,128)(2,1)S(1)}, u32[]{:S(2)}, u32[]{:S(2)}) collective-permute-start(bf16[64,2048]{1,0:T(8,128)(2,1)S(1)} %collective-permute-done.5.rest_6_), channel_id=1, source_target_pairs={{0,8},{4,12},{8,0},{12,4},{16,24},{20,28},{24,16},{28,20},{1,9},{5... | collective-permute-start | bytes 786440 | tf_op jit(solution)/shard_map/ppermute | solution.py:183
  19.5 0.0 collective-permute-start.1
  19.5 3.0 %collective-permute-done.2.rest_2_ = bf16[32,2048]{1,0:T(8,128)(2,1)S(1)} collective-permute-done((bf16[32,2048]{1,0:T(8,128)(2,1)S(1)}, bf16[32,2048]{1,0:T(8,128)(2,1)S(1)}, u32[]{:S(2)}, u32[]{:S(2)}) %collective-permute-start.2) | collective-permute-done | bytes 131104 | tf_op jit(solution)/shard_map/ppermute | solution.py:192
  22.5 0.0 collective-permute-start.3
  22.5 0.0 collective-permute-done.4.rest_5_
  22.5 0.0 collective-permute-done.1.rest_1_
  22.5 1.3 %collective-permute-done.3.rest_3_ = bf16[32,2048]{1,0:T(8,128)(2,1)S(1)} collective-permute-done((bf16[32,2048]{1,0:T(8,128)(2,1)S(1)}, bf16[32,2048]{1,0:T(8,128)(2,1)S(1)}, u32[]{:S(2)}, u32[]{:S(2)}) %collective-permute-start.3) | collective-permute-done | bytes 131104 | tf_op jit(solution)/shard_map/ppermute | solution.py:194
  23.9 2.0 %collective-permute-done.6.rest_7_ = bf16[64,2048]{1,0:T(8,128)(2,1)S(1)} collective-permute-done((bf16[64,2048]{1,0:T(8,128)(2,1)S(1)}, bf16[64,2048]{1,0:T(8,128)(2,1)S(1)}, u32[]{:S(2)}, u32[]{:S(2)}) %collective-permute-start.6) | collective-permute-done | bytes 262176 | tf_op jit(solution)/shard_map/ppermute | solution.py:183
  25.9 1.1 %scores.1 = (f32[64,128]{1,0:T(8,128)S(1)}, f32[64,128]{1,0:T(8,128)S(1)}, f32[64,128]{1,0:T(8,128)S(1)}, f32[64,128]{1,0:T(8,128)S(1)}) custom-call(s32[4]{0:T(128)S(1)} %pad_add_fusion.place, bf16[32,2048]{1,0:T(8,128)(2,1)S(1)} %features.1.rest_0_, bf16[32,2048]{1,0:T(8,128)(2,1)S(1)} %collective-permute-done.1.rest_1_, ...), custom_call_target="tpu_custom_call" | custom-call | tf_op jit(solution)/shard_map/scores/pallas_call | solution.py:146
  27.0 1.5 %collective-permute-start.10 = (f32[64,128]{1,0:T(8,128)S(1)}, f32[64,128]{1,0:T(8,128)S(1)}, u32[]{:S(2)}, u32[]{:S(2)}) collective-permute-start(f32[64,128]{1,0:T(8,128)S(1)} %get-tuple-element.16), channel_id=1, source_target_pairs={{0,16},{2,0},{4,20},{6,4},{8,24},{10,8},{12,28},{14,12},{16,18},{1... | collective-permute-start | bytes 98312 | tf_op jit(solution)/shard_map/ppermute | solution.py:207
  28.6 2.2 %collective-permute-start.7 = (f32[64,128]{1,0:T(8,128)S(1)}, f32[64,128]{1,0:T(8,128)S(1)}, u32[]{:S(2)}, u32[]{:S(2)}) collective-permute-start(f32[64,128]{1,0:T(8,128)S(1)} %get-tuple-element.13), channel_id=1, source_target_pairs={{0,8},{2,24},{4,12},{6,28},{8,0},{10,16},{12,4},{14,20},{16,10},{1... | collective-permute-start | bytes 98312 | tf_op jit(solution)/shard_map/ppermute | solution.py:207
  30.8 1.6 %collective-permute-start.8 = (f32[64,128]{1,0:T(8,128)S(1)}, f32[64,128]{1,0:T(8,128)S(1)}, u32[]{:S(2)}, u32[]{:S(2)}) collective-permute-start(f32[64,128]{1,0:T(8,128)S(1)} %get-tuple-element.14), channel_id=1, source_target_pairs={{0,24},{2,8},{4,28},{6,12},{8,16},{10,0},{12,20},{14,4},{16,26},{1... | collective-permute-start | bytes 98312 | tf_op jit(solution)/shard_map/ppermute | solution.py:207
  32.4 2.4 %collective-permute-start.9 = (f32[64,128]{1,0:T(8,128)S(1)}, f32[64,128]{1,0:T(8,128)S(1)}, u32[]{:S(2)}, u32[]{:S(2)}) collective-permute-start(f32[64,128]{1,0:T(8,128)S(1)} %get-tuple-element.15), channel_id=1, source_target_pairs={{2,16},{6,20},{10,24},{14,28},{16,2},{20,6},{24,10},{28,14},{3,17}... | collective-permute-start | bytes 98312 | tf_op jit(solution)/shard_map/ppermute | solution.py:207
  34.8 0.0 collective-permute-done.10
  34.9 0.3 collective-permute-done.7
  35.2 1.3 %collective-permute-done.8 = f32[64,128]{1,0:T(8,128)S(1)} collective-permute-done((f32[64,128]{1,0:T(8,128)S(1)}, f32[64,128]{1,0:T(8,128)S(1)}, u32[]{:S(2)}, u32[]{:S(2)}) %collective-permute-start.8) | collective-permute-done | bytes 32800 | tf_op jit(solution)/shard_map/ppermute | solution.py:207
  36.5 3.7 %collective-permute-done.9 = f32[64,128]{1,0:T(8,128)S(1)} collective-permute-done((f32[64,128]{1,0:T(8,128)S(1)}, f32[64,128]{1,0:T(8,128)S(1)}, u32[]{:S(2)}, u32[]{:S(2)}) %collective-permute-start.9) | collective-permute-done | bytes 32800 | tf_op jit(solution)/shard_map/ppermute | solution.py:207
  40.3 0.6 %maximum_bitcast_fusion = f32[256,64]{0,1:T(8,128)} fusion(f32[64,128]{1,0:T(8,128)S(1)} %broadcast_select_fusion, f32[64,128]{1,0:T(8,128)S(1)} %get-tuple-element.17), kind=kLoop, calls=%fused_computation | loop fusion | flops 16384 | bytes 131072 | tf_op jit(solution)/shard_map/transpose | solution.py:218
  (2 shorter events, 0.0 us)
Async XLA Ops:
  0.0 11.3 %copy-start = (bf16[64,2048]{1,0:T(8,128)(2,1)S(1)}, bf16[64,2048]{1,0:T(8,128)(2,1)}, u32[]{:S(2)}) copy-start(bf16[64,2048]{1,0:T(8,128)(2,1)} %rest_4_.1) | copy-start | bytes 786436
  0.0 16.2 %copy-start.1 = (s32[1,1024]{1,0:T(1,128)S(1)}, s32[1,1024]{1,0:T(1,128)}, u32[]{:S(2)}) copy-start(s32[1,1024]{1,0:T(1,128)} %segment.1) | copy-start | bytes 12292
  0.0 19.1 %collective-permute-start.5 = (bf16[64,2048]{1,0:T(8,128)(2,1)}, bf16[64,2048]{1,0:T(8,128)(2,1)S(1)}, u32[]{:S(2)}, u32[]{:S(2)}) collective-permute-start(bf16[64,2048]{1,0:T(8,128)(2,1)} %rest_4_.1), channel_id=1, source_target_pairs={{0,16},{4,20},{8,24},{12,28},{16,0},{20,4},{24,8},{28,12},{1,17},{... | collective-permute-start | bytes 786440 | tf_op jit(solution)/shard_map/ppermute | solution.py:180
  9.7 6.4 %collective-permute-start = (bf16[96,1024]{1,0:T(8,128)(2,1)S(1)}, bf16[96,1024]{1,0:T(8,128)(2,1)S(1)}, u32[]{:S(2)}, u32[]{:S(2)}) collective-permute-start(bf16[96,1024]{1,0:T(8,128)(2,1)S(1)} %bitcast.11), channel_id=1, source_target_pairs={{0,2},{2,0},{1,3},{3,1},{4,6},{6,4},{5,7},{7,5},{8,10},{10,8},{9,1... | collective-permute-start | bytes 589832 | tf_op jit(solution)/shard_map/ppermute | solution.py:187
  11.3 11.2 %collective-permute-start.4 = (bf16[64,2048]{1,0:T(8,128)(2,1)S(1)}, bf16[64,2048]{1,0:T(8,128)(2,1)S(1)}, u32[]{:S(2)}, u32[]{:S(2)}) collective-permute-start(bf16[64,2048]{1,0:T(8,128)(2,1)S(1)} %copy-done), channel_id=1, source_target_pairs={{0,8},{4,12},{8,0},{12,4},{16,24},{20,28},{24,16},{28,20},{1,9},{5... | collective-permute-start | bytes 786440 | tf_op jit(solution)/shard_map/ppermute | solution.py:183
  17.5 5.0 %collective-permute-start.2 = (bf16[32,2048]{1,0:T(8,128)(2,1)S(1)}, bf16[32,2048]{1,0:T(8,128)(2,1)S(1)}, u32[]{:S(2)}, u32[]{:S(2)}) collective-permute-start(bf16[32,2048]{1,0:T(8,128)(2,1)S(1)} %features.1.rest_0_), channel_id=1, source_target_pairs={{0,4},{4,0},{8,12},{12,8},{16,20},{20,16},{24,28},{28,24},{1,5},{5... | collective-permute-start | bytes 393224 | tf_op jit(solution)/shard_map/ppermute | solution.py:192
  19.1 6.8 %collective-permute-start.6 = (bf16[64,2048]{1,0:T(8,128)(2,1)S(1)}, bf16[64,2048]{1,0:T(8,128)(2,1)S(1)}, u32[]{:S(2)}, u32[]{:S(2)}) collective-permute-start(bf16[64,2048]{1,0:T(8,128)(2,1)S(1)} %collective-permute-done.5.rest_6_), channel_id=1, source_target_pairs={{0,8},{4,12},{8,0},{12,4},{16,24},{20,28},{24,16},{28,20},{1,9},{5... | collective-permute-start | bytes 786440 | tf_op jit(solution)/shard_map/ppermute | solution.py:183
  19.5 3.0 %collective-permute-start.1 = (bf16[32,2048]{1,0:T(8,128)(2,1)S(1)}, bf16[32,2048]{1,0:T(8,128)(2,1)S(1)}, u32[]{:S(2)}, u32[]{:S(2)}) collective-permute-start(bf16[32,2048]{1,0:T(8,128)(2,1)S(1)} %features.1.rest_0_), channel_id=1, source_target_pairs={{0,1},{1,0},{2,3},{3,2},{4,5},{5,4},{6,7},{7,6},{8,9},{9,8},{10,11... | collective-permute-start | bytes 393224 | tf_op jit(solution)/shard_map/ppermute | solution.py:194
  22.5 1.3 %collective-permute-start.3 = (bf16[32,2048]{1,0:T(8,128)(2,1)S(1)}, bf16[32,2048]{1,0:T(8,128)(2,1)S(1)}, u32[]{:S(2)}, u32[]{:S(2)}) collective-permute-start(bf16[32,2048]{1,0:T(8,128)(2,1)S(1)} %collective-permute-done.2.rest_2_), channel_id=1, source_target_pairs={{0,1},{1,0},{2,3},{3,2},{4,5},{5,4},{6,7},{7,6},{8,9},{9,8},{10,11... | collective-permute-start | bytes 393224 | tf_op jit(solution)/shard_map/ppermute | solution.py:194
  27.0 7.8 %collective-permute-start.10 = (f32[64,128]{1,0:T(8,128)S(1)}, f32[64,128]{1,0:T(8,128)S(1)}, u32[]{:S(2)}, u32[]{:S(2)}) collective-permute-start(f32[64,128]{1,0:T(8,128)S(1)} %get-tuple-element.16), channel_id=1, source_target_pairs={{0,16},{2,0},{4,20},{6,4},{8,24},{10,8},{12,28},{14,12},{16,18},{1... | collective-permute-start | bytes 98312 | tf_op jit(solution)/shard_map/ppermute | solution.py:207
  28.6 6.6 %collective-permute-start.7 = (f32[64,128]{1,0:T(8,128)S(1)}, f32[64,128]{1,0:T(8,128)S(1)}, u32[]{:S(2)}, u32[]{:S(2)}) collective-permute-start(f32[64,128]{1,0:T(8,128)S(1)} %get-tuple-element.13), channel_id=1, source_target_pairs={{0,8},{2,24},{4,12},{6,28},{8,0},{10,16},{12,4},{14,20},{16,10},{1... | collective-permute-start | bytes 98312 | tf_op jit(solution)/shard_map/ppermute | solution.py:207
  30.8 5.7 %collective-permute-start.8 = (f32[64,128]{1,0:T(8,128)S(1)}, f32[64,128]{1,0:T(8,128)S(1)}, u32[]{:S(2)}, u32[]{:S(2)}) collective-permute-start(f32[64,128]{1,0:T(8,128)S(1)} %get-tuple-element.14), channel_id=1, source_target_pairs={{0,24},{2,8},{4,28},{6,12},{8,16},{10,0},{12,20},{14,4},{16,26},{1... | collective-permute-start | bytes 98312 | tf_op jit(solution)/shard_map/ppermute | solution.py:207
  32.4 7.8 %collective-permute-start.9 = (f32[64,128]{1,0:T(8,128)S(1)}, f32[64,128]{1,0:T(8,128)S(1)}, u32[]{:S(2)}, u32[]{:S(2)}) collective-permute-start(f32[64,128]{1,0:T(8,128)S(1)} %get-tuple-element.15), channel_id=1, source_target_pairs={{2,16},{6,20},{10,24},{14,28},{16,2},{20,6},{24,10},{28,14},{3,17}... | collective-permute-start | bytes 98312 | tf_op jit(solution)/shard_map/ppermute | solution.py:207
